TPU v7x, 32 devices: a whole 2x2x4 slice. The times are simulated.
32 devices in a mesh: section: 4 (over x, core), sp: 8 (over z, y).
Axes of the slice: x: 2, y: 2, z: 4, core: 2. Of those that a mesh axis runs over, the one named last changes fastest.
Arguments:
- field_in: bfloat16 [4, 384, 192, 768], P('section', 'sp'), may hold values from -6 to 6
- spectral_gain: bfloat16 [4, 192], P('section'), may hold values from 0.5 to 1.5
- spectral_weight: bfloat16 [4, 384, 192, 384], P('section', 'sp'), may hold values from -0.3125 to 0.3125
- mixer_gain: bfloat16 [4, 192], P('section'), may hold values from 0.5 to 1.5
- up_weight: bfloat16 [4, 192, 384], P('section'), may hold values from -0.4375 to 0.4375
- up_bias: bfloat16 [4, 384], P('section'), may hold values from -3 to 3
- down_weight: bfloat16 [4, 192, 384], P('section'), may hold values from -0.3125 to 0.3125
Outputs:
- next_field: bfloat16 [4, 384, 192, 768], P('section', 'sp')
All inputs are finite; a program needn't handle non-finite values.
Results may differ from a plain program's by a relative error of at most 0.012.
Values may be sent and summed in bfloat16 or wider, within the bound.
A program may use at most 192 MiB of HBM per device.

v0:
```python
import math
import jax
import jax.numpy as jnp
from jax import lax
from jax.sharding import PartitionSpec as P

C = 192
NLAT = 384
NLON = 768
LMAX = 384
MMAX = 384
CHUNKS = 4
EPSILON = 1e-05


def passed_along(value, axis, by):
    count = lax.axis_size(axis)
    return lax.ppermute(value, axis, [(i, (i + by) % count) for i in range(count)])


def quad_weights(cycle_index, cycle_count):
    terms_count = cycle_count // 2
    orders = jnp.arange(1, terms_count + 1, dtype=jnp.int32)
    phase_turns = orders[None, :] * (2 * cycle_index[:, None] + 1) % (2 * cycle_count)
    angles = math.pi * phase_turns.astype(jnp.float32) / cycle_count
    orders_real = orders.astype(jnp.float32)
    series = jnp.sum(jnp.cos(angles) / (4.0 * orders_real * orders_real - 1.0)[None, :], axis=1)
    return 2.0 / cycle_count * (1.0 - 2.0 * series)


def fourier_tables(point_count, orders):
    points = jnp.arange(point_count, dtype=jnp.int32)
    phase_turns = points[:, None] * orders[None, :] % point_count
    angles = 2.0 * math.pi / point_count * phase_turns.astype(jnp.float32)
    cosines = jnp.cos(angles)
    sine_values = jnp.sin(angles)
    forward = jnp.stack([cosines, -sine_values], axis=1).astype(jnp.bfloat16)
    doubling = jnp.where(orders == 0, 1.0, 2.0).astype(jnp.float32)[:, None]
    inverse = jnp.stack([cosines.T * doubling, -sine_values.T * doubling], axis=0).astype(
        jnp.bfloat16
    )
    return (forward, inverse)


def step_entries(degree, order_col, cosines):
    active = degree >= order_col + 1.0
    further = degree >= order_col + 2.0
    degree_sq = degree * degree
    order_sq = order_col * order_col
    lead_coeff = jnp.sqrt(
        jnp.where(
            active, (4.0 * degree_sq - 1.0) / jnp.where(active, degree_sq - order_sq, 1.0), 0.0
        )
    )
    before = degree - 1.0
    before_sq = before * before
    trail_coeff = jnp.sqrt(
        jnp.where(
            further, (before_sq - order_sq) / jnp.where(further, 4.0 * before_sq - 1.0, 1.0), 0.0
        )
    )
    diag_top = jnp.where(active, lead_coeff * cosines, 1.0)
    off_top = jnp.where(active, -lead_coeff * trail_coeff, 0.0)
    off_low = jnp.where(active, 1.0, 0.0)
    diag_low = jnp.where(active, 0.0, 1.0)
    return (diag_top, off_top, off_low, diag_low)


def legendre_rows(order_index, cycle_count, degree_count):
    colatitude = math.pi * (jnp.arange(cycle_count, dtype=jnp.float32) + 0.5) / cycle_count
    cosines = jnp.cos(colatitude)[None, None, :]
    sine_values = jnp.sin(colatitude)
    order_real = order_index.astype(jnp.float32)
    steps_all = jnp.arange(1, degree_count + 1, dtype=jnp.float32)
    factors = jnp.log((2.0 * steps_all - 1.0) / (2.0 * steps_all))
    below_mask = (steps_all[None, :] <= order_real[:, None]).astype(jnp.float32)
    partial_log = jnp.sum(below_mask * factors[None, :], axis=1)
    start_log = 0.5 * jnp.log((2.0 * order_real + 1.0) / (4.0 * math.pi)) + 0.5 * partial_log
    start_log = start_log[:, None] + order_real[:, None] * jnp.log(sine_values)[None, :]
    order_col = order_real[None, :, None]
    block_count = degree_count // 16
    block_base = (16 * jnp.arange(block_count, dtype=jnp.int32)).astype(jnp.float32)[:, None, None]
    shape_all = (block_count, order_index.shape[0], cycle_count)
    unit_array = jnp.ones(shape_all, jnp.float32)
    zero_array = jnp.zeros(shape_all, jnp.float32)

    def product_half(half_turn, matrices):
        upper_left, upper_right, lower_left, lower_right, log_scale = matrices
        for inner_step in range(8):
            degree = block_base + (half_turn * 8 + inner_step).astype(jnp.float32)
            diag_top, off_top, off_low, diag_low = step_entries(degree, order_col, cosines)
            next_ul = diag_top * upper_left + off_top * lower_left
            next_ur = diag_top * upper_right + off_top * lower_right
            next_ll = off_low * upper_left + diag_low * lower_left
            next_lr = off_low * upper_right + diag_low * lower_right
            largest = jnp.maximum(
                jnp.maximum(jnp.abs(next_ul), jnp.abs(next_ur)),
                jnp.maximum(jnp.abs(next_ll), jnp.abs(next_lr)),
            )
            upper_left = next_ul / largest
            upper_right = next_ur / largest
            lower_left = next_ll / largest
            lower_right = next_lr / largest
            log_scale = log_scale + jnp.log(largest)
        return (upper_left, upper_right, lower_left, lower_right, log_scale)

    products = lax.fori_loop(
        0, 2, product_half, (unit_array, zero_array, zero_array, unit_array, zero_array)
    )

    def carry_block(vector_state, block_matrix):
        lead_value, lag_value, log_value = vector_state
        upper_left, upper_right, lower_left, lower_right, log_scale = block_matrix
        next_lead = upper_left * lead_value + upper_right * lag_value
        next_lag = lower_left * lead_value + lower_right * lag_value
        largest = jnp.maximum(jnp.abs(next_lead), jnp.abs(next_lag))
        return (
            (next_lead / largest, next_lag / largest, log_value + log_scale + jnp.log(largest)),
            vector_state,
        )

    initial = (unit_array[0], zero_array[0], start_log)
    final_state, starts = lax.scan(carry_block, initial, products)

    def degree_half(vector_state, half_turn):
        lead_value, lag_value, log_value = vector_state
        values = []
        for inner_step in range(8):
            degree = block_base + (half_turn * 8 + inner_step).astype(jnp.float32)
            diag_top, off_top, off_low, diag_low = step_entries(degree, order_col, cosines)
            next_lead = diag_top * lead_value + off_top * lag_value
            next_lag = off_low * lead_value + diag_low * lag_value
            largest = jnp.maximum(jnp.abs(next_lead), jnp.abs(next_lag))
            lead_value = next_lead / largest
            lag_value = next_lag / largest
            log_value = log_value + jnp.log(largest)
            values.append(lead_value * jnp.exp(log_value))
        return ((lead_value, lag_value, log_value), jnp.stack(values))

    last_state, table_rows = lax.scan(degree_half, starts, jnp.arange(2, dtype=jnp.int32))
    legendre = jnp.transpose(table_rows, (3, 2, 0, 1, 4)).reshape(
        order_index.shape[0], degree_count, cycle_count
    )
    degrees = jnp.arange(degree_count, dtype=jnp.int32)
    return jnp.where(degrees[None, :, None] >= order_index[:, None, None], legendre, 0.0)


def layer_norm(values, gain_row):
    values = values.astype(jnp.float32)
    average = jnp.mean(values, axis=-2, keepdims=True)
    centred = values - average
    variance = jnp.mean(centred * centred, axis=-2, keepdims=True)
    return centred * lax.rsqrt(variance + EPSILON) * gain_row.astype(jnp.float32)[:, None]


def mixing_matrix(weight):
    width = weight.shape[1]
    real_weight = weight[:, :, :width]
    imag_weight = weight[:, :, width:]
    top_half = jnp.concatenate([real_weight, imag_weight], axis=2)
    bottom_half = jnp.concatenate([-imag_weight, real_weight], axis=2)
    return jnp.concatenate([top_half, bottom_half], axis=1)


def order_list(sp_count, modes_dev):
    slots = jnp.arange(MMAX, dtype=jnp.int32)
    owner = slots // modes_dev
    within = slots % modes_dev
    mirrored = jnp.where(within % 2 == 0, owner, sp_count - 1 - owner)
    return within * sp_count + mirrored


def triangle_plan(sp_count, half):
    plan = []
    for rank in range(sp_count):
        low_block = min(rank, sp_count - 1 - rank)
        high_block = sp_count - 1 - low_block
        low_half = 0 if rank == low_block else 1
        low_start = (2 * low_block + low_half) * half
        high_start = (2 * high_block + 1 - low_half) * half
        low_count = (low_start + half - 1) // sp_count + 1
        high_count = (high_start + half - 1) // sp_count + 1
        plan.append((low_start, low_count, high_start, high_count))
    slots = max((entry[1] + entry[3] for entry in plan))
    return (plan, slots)


def shards(field_in, spectral_gain, spectral_weight, mixer_gain, up_weight, up_bias, down_weight):
    grid_values = field_in[0]
    cycle_rows = grid_values.shape[0]
    sp_count = lax.axis_size("sp")
    device_rank = lax.axis_index("sp")
    modes_dev = MMAX // sp_count
    all_orders = order_list(sp_count, modes_dev)
    order_index = lax.dynamic_slice_in_dim(all_orders, device_rank * modes_dev, modes_dev, 0)
    cycle_index = device_rank * cycle_rows + jnp.arange(cycle_rows, dtype=jnp.int32)
    legendre = legendre_rows(order_index, NLAT, LMAX).astype(jnp.bfloat16)
    forward, inverse = fourier_tables(NLON, all_orders)
    weighting = quad_weights(cycle_index, NLAT) * (2.0 * math.pi / NLON)
    normed = layer_norm(grid_values, spectral_gain[0]).astype(jnp.bfloat16)
    spectral = jnp.einsum("nrm,acn->marc", forward, normed, preferred_element_type=jnp.float32)
    spectral = (
        (spectral * weighting[None, :, None, None])
        .astype(jnp.bfloat16)
        .reshape(MMAX, cycle_rows, 2 * C)
    )
    coeffs = jnp.einsum(
        "mla,mak->mlk",
        legendre,
        lax.all_to_all(spectral, "sp", split_axis=0, concat_axis=1, tiled=True),
        preferred_element_type=jnp.float32,
    ).astype(jnp.bfloat16)
    half = LMAX // sp_count // 2
    plan, slots = triangle_plan(sp_count, half)
    own_weight = spectral_weight[0]
    partner = [(i, sp_count - 1 - i) for i in range(sp_count)]
    other_weight = lax.ppermute(own_weight[half:], "sp", partner)
    is_low = device_rank < sp_count // 2
    low_weight = mixing_matrix(jnp.where(is_low, own_weight[:half], other_weight))
    high_weight = mixing_matrix(jnp.where(is_low, other_weight, own_weight[:half]))
    width = coeffs.shape[2]
    pieces = []
    for low_start, low_count, high_start, high_count in plan:
        pieces.append(coeffs[:low_count, low_start : low_start + half])
        gap = slots - low_count - high_count
        if gap:
            pieces.append(jnp.zeros((gap, half, width), coeffs.dtype))
        pieces.append(coeffs[:high_count, high_start : high_start + half])
    packed = jnp.concatenate(pieces, axis=0)
    by_degree = lax.all_to_all(packed, "sp", split_axis=0, concat_axis=0, tiled=True)
    by_degree = by_degree.reshape(sp_count, slots, half, width)
    most_low = max((entry[1] for entry in plan))
    most_high = max((entry[3] for entry in plan))
    low_mixed = jnp.einsum(
        "dslk,lkj->dslj", by_degree[:, :most_low], low_weight, preferred_element_type=jnp.float32
    ).astype(jnp.bfloat16)
    high_mixed = jnp.einsum(
        "dslk,lkj->dslj",
        by_degree[:, slots - most_high :],
        high_weight,
        preferred_element_type=jnp.float32,
    ).astype(jnp.bfloat16)
    low_rows = jnp.array([entry[1] for entry in plan], jnp.int32)[device_rank]
    row = jnp.arange(slots, dtype=jnp.int32)[None, :, None, None]
    mixed = jnp.where(
        row < low_rows,
        jnp.pad(low_mixed, ((0, 0), (0, slots - most_low), (0, 0), (0, 0))),
        jnp.pad(high_mixed, ((0, 0), (slots - most_high, 0), (0, 0), (0, 0))),
    )
    returned = lax.all_to_all(
        mixed.reshape(sp_count * slots, half, width), "sp", split_axis=0, concat_axis=0, tiled=True
    ).reshape(sp_count, slots, half, width)
    parts = {}
    for rank, (low_start, low_count, high_start, high_count) in enumerate(plan):
        parts[low_start] = (returned[rank, :low_count], low_count)
        parts[high_start] = (returned[rank, slots - high_count :], high_count)
    mixed_coeffs = jnp.concatenate(
        [
            jnp.pad(parts[start][0], ((0, modes_dev - parts[start][1]), (0, 0), (0, 0)))
            for start in sorted(parts)
        ],
        axis=1,
    )
    grid_part = jnp.einsum(
        "mla,mlk->mak", legendre, mixed_coeffs, preferred_element_type=jnp.float32
    ).astype(jnp.bfloat16)
    grid_part = grid_part.reshape(modes_dev, sp_count, cycle_rows, width)
    chunk = cycle_rows // CHUNKS
    outputs = []
    for start in range(0, cycle_rows, chunk):
        on_grid = lax.all_to_all(
            grid_part[:, :, start : start + chunk].reshape(modes_dev, sp_count * chunk, width),
            "sp",
            split_axis=1,
            concat_axis=0,
            tiled=True,
        )
        synthesis = jnp.einsum(
            "marc,rmn->acn",
            on_grid.reshape(MMAX, chunk, 2, C),
            inverse,
            preferred_element_type=jnp.float32,
        )
        residual = grid_values[start : start + chunk].astype(jnp.float32) + synthesis
        hidden_in = layer_norm(residual, mixer_gain[0]).astype(jnp.bfloat16)
        hidden = jnp.einsum(
            "acn,ch->anh", hidden_in, up_weight[0], preferred_element_type=jnp.float32
        ) + up_bias[0].astype(jnp.float32)
        hidden = jax.nn.gelu(hidden, approximate=False).astype(jnp.bfloat16)
        branch = jnp.einsum(
            "anh,ch->acn", hidden, down_weight[0], preferred_element_type=jnp.float32
        )
        result = (residual + branch).astype(jnp.bfloat16)
        outputs.append(passed_along(result, "section", 1))
    return jnp.concatenate(outputs, axis=0)[None]


def solution(mesh):
    in_specs = (
        P("section", "sp", None, None),
        P("section", None),
        P("section", "sp", None, None),
        P("section", None),
        P("section", None, None),
        P("section", None),
        P("section", None, None),
    )
    out_specs = P("section", "sp", None, None)
    return jax.shard_map(shards, mesh=mesh, in_specs=in_specs, out_specs=out_specs, check_vma=False)
```

profile of v0, /device:TPU:0, one launch (start us, length us, event | category | flops | bytes accessed | tf_op | source)
XLA Modules:
  0.0 1701.2 jit_solution(16613426593756830060)
XLA Ops:
  1.2 7.8 convert_reduce_fusion
  9.0 10.3 fusion.183
  24.8 19.0 %multiply_convert_fusion = bf16[48,192,2,384]{3,1,2,0:T(8,128)(2,1)} fusion(f32[48]{0:T(128)S(1)} %subtract_multiply_fusion, bf16[1,48,192,768]{3,2,1,0:T(8,128)(2,1)} %param.14, f32[192]{0:T(256)S(1)} %bitcast.620, f32[48,768]{1,0:T(8,128)S(1)} %add_rsqrt_fusion, f32[48,768]{1,0:T(8,128)S(1)} %broadcast_multiply_fusion, ...), kind=kOutput, calls=%fused_computation.485 | convolution fusion | flops 10923540480 | bytes 29787072 | tf_op jit(solution)/shard_map/nrm,acn->marc/dot_general | solution.py:201
  43.8 18.6 %copy.34 = bf16[384,48,384]{2,1,0:T(8,128)(2,1)} copy(bf16[384,48,384]{0,2,1:T(8,128)(2,1)} %bitcast.601) | data formatting | bytes 28311552 | tf_op jit(solution)/shard_map/reshape | solution.py:205
  62.4 7.3 all-to-all-start
  72.0 59.7 %while.70 = (s32[]{:T(128)}, f32[24,48,384]{2,1,0:T(8,128)}, f32[24,48,384]{2,1,0:T(8,128)}, f32[24,48,384]{2,1,0:T(8,128)}, f32[24,48,384]{2,1,0:T(8,128)}, /*i...) while((s32[]{:T(128)}, f32[24,48,384]{2,1,0:T(8,128)}, ...), condition=%wide.region_2.3_spmd.clone.clone, body=%wide.region_1.2_spmd.clone.clone.sunk | while | flops 123129520 | bytes 200388496 | solution.py:107
  132.4 58.0 %while.69 = (s32[]{:T(128)}, f32[48,384]{1,0:T(8,128)S(1)}, f32[48,384]{1,0:T(8,128)S(1)}, f32[48,384]{1,0:T(8,128)S(1)}, f32[24,48,384]{2,1,0:T(8,128)}, /*inde...) while((s32[]{:T(128)}, f32[48,384]{1,0:T(8,128)S(1)}, ...), condition=%wide.region_4.5_spmd.clone, body=%wide.region_3.4_spmd.clone.sunk | while | flops 368643 | bytes 1548453 | solution.py:123
  190.5 100.2 %while.68 = (s32[]{:T(128)}, f32[24,48,384]{2,1,0:T(8,128)}, f32[24,48,384]{2,1,0:T(8,128)}, f32[24,48,384]{2,1,0:T(8,128)S(1)}, bf16[2,8,24,48,384]{4,1,0,2,3:T...) while((s32[]{:T(128)}, f32[24,48,384]{2,1,0:T(8,128)}, ...), condition=%wide.region_6.7_spmd.clone.clone, body=%wide.region_5.6_spmd.clone.clone.sunk | while | flops 100568752 | bytes 101660528 | solution.py:140
  211.3 7.1 bitcast_dynamic-update-slice_fusion.25
  220.7 7.1 bitcast_dynamic-update-slice_fusion.27
  233.5 7.2 copy_dynamic-update-slice_fusion.2
  261.3 7.1 bitcast_dynamic-update-slice_fusion.25
  270.7 7.1 bitcast_dynamic-update-slice_fusion.27
  283.5 7.2 copy_dynamic-update-slice_fusion.2
  290.7 14.3 fusion.186
  305.0 71.5 %all-to-all-done = bf16[384,48,384]{2,1,0:T(8,128)(2,1)} async-done(((bf16[384,48,384]{2,1,0:T(8,128)(2,1)}), bf16[384,48,384]{2,1,0:T(8,128)(2,1)}, u32[]{:S(2)}, u32[]{:S(2)}) %all-to-all-start) | async-done | bytes 14155808 | tf_op jit(solution)/shard_map/all_to_all | solution.py:210
  376.5 12.9 copy.35
  389.4 19.7 %convolution_convert_fusion.1 = bf16[48,384,384]{2,1,0:T(8,128)(2,1)} fusion(bf16[48,384,384]{2,1,0:T(8,128)(2,1)} %fusion.186, bf16[48,384,384]{2,1,0:T(8,128)(2,1)} %bitcast.579), kind=kOutput, calls=%fused_computation.578 | convolution fusion | flops 5442895872 | bytes 42467328 | tf_op jit(solution)/shard_map/mla,mak->mlk/dot_general | solution.py:207
  453.3 191.3 %collective-permute-done = bf16[24,192,384]{2,1,0:T(8,128)(2,1)} collective-permute-done((bf16[24,192,384]{2,1,0:T(8,128)(2,1)}, bf16[24,192,384]{2,1,0:T(8,128)(2,1)}, u32[]{:S(2)}, u32[]{:S(2)}) %collective-permute-start) | collective-permute-done | bytes 3538976 | tf_op jit(solution)/shard_map/ppermute | solution.py:217
  655.4 29.7 %all-to-all-done.1 = bf16[408,24,384]{2,1,0:T(8,128)(2,1)} async-done(((bf16[408,24,384]{2,1,0:T(8,128)(2,1)}), bf16[408,24,384]{2,1,0:T(8,128)(2,1)}, u32[]{:S(2)}, u32[]{:S(2)}) %all-to-all-start.1) | async-done | bytes 7520288 | tf_op jit(solution)/shard_map/all_to_all | solution.py:230
  697.1 15.2 fusion.237
  712.3 8.9 convert_bitcast_fusion.1
  731.8 12.0 pad_select_fusion
  743.8 7.9 copy.38
  751.7 252.8 %all_to_all.88 = bf16[408,24,384]{2,1,0:T(8,128)(2,1)S(1)} all-to-all(bf16[408,24,384]{2,1,0:T(8,128)(2,1)S(1)} %bitcast.596), channel_id=1, replica_groups=mesh['section'=4,'sp'=8] {'sp'}, dimensions={0} | all-to-all | bytes 15040512 | tf_op jit(solution)/shard_map/all_to_all | solution.py:250
  1021.1 19.2 %convolution_convert_fusion = bf16[48,384,384]{2,1,0:T(8,128)(2,1)} fusion(bf16[48,384,384]{2,1,0:T(8,128)(2,1)} %fusion.186, bf16[48,384,384]{2,1,0:T(8,128)(2,1)} %fusion.307), kind=kOutput, calls=%fused_computation.577 | convolution fusion | flops 5442895872 | bytes 42467328 | tf_op jit(solution)/shard_map/mla,mlk->mak/dot_general | solution.py:264
  1040.3 14.2 fusion.482
  1069.2 72.0 %all-to-all-done.5 = bf16[48,96,384]{2,0,1:T(8,128)(2,1)} async-done(((bf16[48,96,384]{2,0,1:T(8,128)(2,1)}), bf16[48,96,384]{2,0,1:T(8,128)(2,1)}, u32[]{:S(2)}, u32[]{:S(2)}) %all-to-all-start.5) | async-done | bytes 3538976 | tf_op jit(solution)/shard_map/all_to_all | solution.py:271
  1152.4 71.9 %all-to-all-done.3 = bf16[48,96,384]{2,0,1:T(8,128)(2,1)} async-done(((bf16[48,96,384]{2,0,1:T(8,128)(2,1)}), bf16[48,96,384]{2,0,1:T(8,128)(2,1)}, u32[]{:S(2)}, u32[]{:S(2)}) %all-to-all-start.3) | async-done | bytes 3538976 | tf_op jit(solution)/shard_map/all_to_all | solution.py:271
  1235.0 72.4 %all-to-all-done.6 = bf16[48,96,384]{2,0,1:T(8,128)(2,1)} async-done(((bf16[48,96,384]{2,0,1:T(8,128)(2,1)}), bf16[48,96,384]{2,0,1:T(8,128)(2,1)}, u32[]{:S(2)}, u32[]{:S(2)}) %all-to-all-start.6) | async-done | bytes 3538976 | tf_op jit(solution)/shard_map/all_to_all | solution.py:271
  1317.6 9.5 copy.61
  1327.2 12.9 reshape.7129
  1340.1 9.5 copy.58
  1349.7 13.0 reshape.7126
  1362.6 9.5 copy.60
  1372.1 13.1 reshape.7128
  1413.7 9.5 copy.59
  1423.2 13.1 reshape.7127
  1446.2 6.9 fusion.264
  1459.6 6.9 fusion.266
  1466.4 32.9 %fusion.251 = (u16[768,384]{1,0:T(8,128)(2,1)S(1)}, u16[768,384]{1,0:T(8,128)(2,1)S(1)}, u16[768,384]{1,0:T(8,128)(2,1)S(1)}, u16[768,384]{1,0:T(8,128)(2,1)S(1)...) fusion(f32[384]{0:T(512)S(1)} %convert_reduce_fusion.1, ...), kind=kOutput, calls=%fused_computation.617 | convolution fusion | flops 1561853952 | bytes 68643072 | tf_op jit(solution)/shard_map/acn,ch->anh/dot_general | solution.py:286
  1499.3 37.1 %fusion.246 = bf16[12,192,768]{2,1,0:T(8,128)(2,1)} fusion(f32[12,192,768]{2,1,0:T(8,128)} %copy-done.21, f32[12,768,384]{2,1,0:T(8,128)} %get-tuple-element.1155, f32[384]{0:T(512)S(1)} %convert_reduce_fusion.1, u16[768,384]{1,0:T(8,128)(2,1)S(1)} %get-tuple-element.775, u16[768,384]{1,0:T(8,128)(2,1)S(1)} %get-tuple-element.774, ...), kind=kOutput, calls=%fused_computation.603 | convolution fusion | flops 1613758464 | bytes 26101248 | tf_op jit(solution)/shard_map/anh,ch->acn/dot_general | solution.py:290
  1536.5 37.0 %fusion.243 = bf16[12,192,768]{2,1,0:T(8,128)(2,1)} fusion(f32[12,192,768]{2,1,0:T(8,128)} %copy-done.8, f32[12,768,384]{2,1,0:T(8,128)S(1)} %copy-done.18, f32[384]{0:T(512)S(1)} %convert_reduce_fusion.1, u16[768,384]{1,0:T(8,128)(2,1)S(1)} %get-tuple-element.782, u16[768,384]{1,0:T(8,128)(2,1)S(1)} %get-tuple-element.783, ...), kind=kOutput, calls=%fused_computation.597 | convolution fusion | flops 1613758464 | bytes 26101248 | tf_op jit(solution)/shard_map/anh,ch->acn/dot_general | solution.py:290
  1575.0 36.2 %fusion.244 = bf16[12,192,768]{2,1,0:T(8,128)(2,1)} fusion(f32[12,192,768]{2,1,0:T(8,128)S(1)} %copy-done.10, f32[12,768,384]{2,1,0:T(8,128)S(1)} %copy-done.17, f32[384]{0:T(512)S(1)} %convert_reduce_fusion.1, u16[768,384]{1,0:T(8,128)(2,1)} %get-tuple-element.784, u16[768,384]{1,0:T(8,128)(2,1)} %get-tuple-element.785, ...), kind=kOutput, calls=%fused_computation.599 | convolution fusion | flops 1613758464 | bytes 26101248 | tf_op jit(solution)/shard_map/anh,ch->acn/dot_general | solution.py:290
  1611.3 33.9 %fusion.245 = bf16[12,192,768]{2,1,0:T(8,128)(2,1)S(1)} fusion(f32[12,192,768]{2,1,0:T(8,128)S(1)} %copy-done.12, f32[12,768,384]{2,1,0:T(8,128)S(1)} %copy-done.16, f32[384]{0:T(512)S(1)} %convert_reduce_fusion.1, u16[768,384]{1,0:T(8,128)(2,1)S(1)} %copy-done.34, u16[768,384]{1,0:T(8,128)(2,1)S(1)} %copy-done.35, bf16[1,192,384]{2,1,0:T(8,128)(2,1)S(1)} %copy-done.32), kind=kOutput, calls=%fused_computation.601 | convolution fusion | flops 1613758464 | bytes 26101248 | tf_op jit(solution)/shard_map/anh,ch->acn/dot_general | solution.py:290
  1645.9 7.5 collective-permute-done.3
  1653.4 37.9 %collective-permute-done.2 = bf16[12,192,768]{2,1,0:T(8,128)(2,1)S(1)} collective-permute-done((bf16[12,192,768]{2,1,0:T(8,128)(2,1)S(1)}, bf16[12,192,768]{2,1,0:T(8,128)(2,1)S(1)}, u32[]{:S(2)}, u32[]{:S(2)}) %collective-permute-start.2) | collective-permute-done | bytes 3538976 | tf_op jit(solution)/shard_map/ppermute | solution.py:18
  1691.3 9.6 maximum_bitcast_fusion
  (454 shorter events, 369.5 us)
Async XLA Ops:
  0.0 1446.2 %copy-start = (bf16[1,192,384]{2,1,0:T(8,128)(2,1)S(1)}, bf16[1,192,384]{2,1,0:T(8,128)(2,1)}, u32[]{:S(2)}) copy-start(bf16[1,192,384]{2,1,0:T(8,128)(2,1)} %param.18) | copy-start | bytes 442372
  0.0 70.3 %copy-start.25 = (s32[384]{0:T(512)}, s32[384]{0:T(512)S(1)}, u32[]{:S(2)}) copy-start(s32[384]{0:T(512)S(1)} %fusion.328) | copy-start | bytes 4612
  62.4 314.1 %all-to-all-start = ((bf16[384,48,384]{2,1,0:T(8,128)(2,1)}), bf16[384,48,384]{2,1,0:T(8,128)(2,1)}, u32[]{:S(2)}, u32[]{:S(2)}) async-start(bf16[384,48,384]{2,1,0:T(8,128)(2,1)} %copy.34), calls=%async_computation | async-start | bytes 28311552 | tf_op jit(solution)/shard_map/all_to_all | solution.py:210
  71.9 59.7 %copy-start.27 = (f32[384]{0:T(512)S(1)}, f32[384]{0:T(512)}, u32[]{:S(2)}) copy-start(f32[384]{0:T(512)} %sine_log_fusion) | copy-start | bytes 4612
  71.9 59.7 %copy-start.31 = (f32[48]{0:T(128)S(1)}, f32[48]{0:T(128)}, u32[]{:S(2)}) copy-start(f32[48]{0:T(128)} %add_multiply_fusion.16) | copy-start | bytes 580
  71.9 60.4 %copy-start.1 = (f32[24,48,384]{2,1,0:T(8,128)S(1)}, f32[24,48,384]{2,1,0:T(8,128)}, u32[]{:S(2)}) copy-start(f32[24,48,384]{2,1,0:T(8,128)} %custom-call.13) | copy-start | bytes 5308420
  71.9 60.4 %copy-start.19 = (f32[48,384]{1,0:T(8,128)S(1)}, f32[48,384]{1,0:T(8,128)}, u32[]{:S(2)}) copy-start(f32[48,384]{1,0:T(8,128)} %custom-call) | copy-start | bytes 221188
  72.0 60.4 %copy-start.20 = (f32[48,384]{1,0:T(8,128)S(1)}, f32[48,384]{1,0:T(8,128)}, u32[]{:S(2)}) copy-start(f32[48,384]{1,0:T(8,128)} %custom-call.1) | copy-start | bytes 221188
  87.6 4.4 copy-start.6
  96.6 3.9 copy-start.7
  101.5 5.5 copy-start.2
  101.5 5.5 copy-start.3
  101.5 5.5 copy-start.4
  101.5 5.5 copy-start.5
  118.6 4.4 copy-start.6
  127.7 3.9 copy-start.7
  190.4 100.2 %copy-start.24 = (pred[48,384]{1,0:T(8,128)(4,1)S(1)}, pred[48,384]{1,0:T(8,128)(4,1)}, u32[]{:S(2)}) copy-start(pred[48,384]{1,0:T(8,128)(4,1)} %iota_compare_fusion) | copy-start | bytes 55300
  438.5 246.6 %all-to-all-start.1 = ((bf16[408,24,384]{2,1,0:T(8,128)(2,1)}), bf16[408,24,384]{2,1,0:T(8,128)(2,1)}, u32[]{:S(2)}, u32[]{:S(2)}) async-start(bf16[408,24,384]{2,1,0:T(8,128)(2,1)} %slice_dynamic-update-slice_fusion.1), calls=%async_computation.1 | async-start | bytes 15040512 | tf_op jit(solution)/shard_map/all_to_all | solution.py:230
  443.4 8.8 copy-start.33
  447.5 197.0 %collective-permute-start = (bf16[24,192,384]{2,1,0:T(8,128)(2,1)}, bf16[24,192,384]{2,1,0:T(8,128)(2,1)}, u32[]{:S(2)}, u32[]{:S(2)}) collective-permute-start(bf16[24,192,384]{2,1,0:T(8,128)(2,1)} %slice_bitcast_fusion), channel_id=1, source_target_pairs={{0,7},{1,6},{2,5},{3,4},{4,3},{5,2},{6,1},{7,0},{8,15},{9,14},{10,... | collective-permute-start | bytes 10616840 | tf_op jit(solution)/shard_map/ppermute | solution.py:217
  1058.4 82.8 %all-to-all-start.5 = ((bf16[48,96,384]{2,0,1:T(8,128)(2,1)}), bf16[48,96,384]{2,0,1:T(8,128)(2,1)}, u32[]{:S(2)}, u32[]{:S(2)}) async-start(bf16[48,96,384]{2,0,1:T(8,128)(2,1)} %bitcast.605), calls=%async_computation.5 | async-start | bytes 7077888 | tf_op jit(solution)/shard_map/all_to_all | solution.py:271
  1141.2 83.0 %all-to-all-start.3 = ((bf16[48,96,384]{2,0,1:T(8,128)(2,1)}), bf16[48,96,384]{2,0,1:T(8,128)(2,1)}, u32[]{:S(2)}, u32[]{:S(2)}) async-start(bf16[48,96,384]{2,0,1:T(8,128)(2,1)} %bitcast.604), calls=%async_computation.3 | async-start | bytes 7077888 | tf_op jit(solution)/shard_map/all_to_all | solution.py:271
  1224.2 83.1 %all-to-all-start.6 = ((bf16[48,96,384]{2,0,1:T(8,128)(2,1)}), bf16[48,96,384]{2,0,1:T(8,128)(2,1)}, u32[]{:S(2)}, u32[]{:S(2)}) async-start(bf16[48,96,384]{2,0,1:T(8,128)(2,1)} %bitcast.603), calls=%async_computation.6 | async-start | bytes 7077888 | tf_op jit(solution)/shard_map/all_to_all | solution.py:271
  1307.4 4.7 copy-start.30
  1307.4 4.7 copy-start.29
  1307.4 4.7 copy-start.26
  1307.4 106.3 %all-to-all-start.4 = ((bf16[48,96,384]{2,0,1:T(8,128)(2,1)}), bf16[48,96,384]{2,0,1:T(8,128)(2,1)}, u32[]{:S(2)}, u32[]{:S(2)}) async-start(bf16[48,96,384]{2,0,1:T(8,128)(2,1)} %bitcast.602), calls=%async_computation.4 | async-start | bytes 7077888 | tf_op jit(solution)/shard_map/all_to_all | solution.py:271
  1391.5 3.6 copy-start.8
  1391.5 4.6 copy-start.23
  1401.2 3.6 copy-start.21
  1401.2 4.6 copy-start.22
  1442.6 3.6 copy-start.11
  1442.6 10.4 slice-start.2
  1446.2 6.9 slice-start.3
  1446.2 13.4 slice-start
  1453.0 6.5 slice-start.1
  1466.4 32.9 %copy-start.32 = (bf16[1,192,384]{2,1,0:T(8,128)(2,1)S(1)}, bf16[1,192,384]{2,1,0:T(8,128)(2,1)}, u32[]{:S(2)}) copy-start(bf16[1,192,384]{2,1,0:T(8,128)(2,1)} %param.20) | copy-start | bytes 442372
  1499.3 37.1 %copy-start.18 = (f32[12,768,384]{2,1,0:T(8,128)S(1)}, f32[12,768,384]{2,1,0:T(8,128)}, u32[]{:S(2)}) copy-start(f32[12,768,384]{2,1,0:T(8,128)} %fusion.266) | copy-start | bytes 42467332
  1536.4 109.5 %collective-permute-start.1 = (bf16[12,192,768]{2,1,0:T(8,128)(2,1)}, bf16[12,192,768]{2,1,0:T(8,128)(2,1)}, u32[]{:S(2)}, u32[]{:S(2)}) collective-permute-start(bf16[12,192,768]{2,1,0:T(8,128)(2,1)} %fusion.246), channel_id=1, source_target_pairs={{0,8},{8,16},{16,24},{24,0},{1,9},{9,17},{17,25},{25,1},{2,10},{10... | collective-permute-start | bytes 10616840 | tf_op jit(solution)/shard_map/ppermute | solution.py:18
  1536.4 38.6 %copy-start.10 = (f32[12,192,768]{2,1,0:T(8,128)S(1)}, f32[12,192,768]{2,1,0:T(8,128)}, u32[]{:S(2)}) copy-start(f32[12,192,768]{2,1,0:T(8,128)} %copy-done.9) | copy-start | bytes 21233668
  1536.4 38.6 %copy-start.17 = (f32[12,768,384]{2,1,0:T(8,128)S(1)}, f32[12,768,384]{2,1,0:T(8,128)}, u32[]{:S(2)}) copy-start(f32[12,768,384]{2,1,0:T(8,128)} %fusion.265) | copy-start | bytes 42467332
  1573.4 72.5 %collective-permute-start.4 = (bf16[12,192,768]{2,1,0:T(8,128)(2,1)}, bf16[12,192,768]{2,1,0:T(8,128)(2,1)}, u32[]{:S(2)}, u32[]{:S(2)}) collective-permute-start(bf16[12,192,768]{2,1,0:T(8,128)(2,1)} %fusion.243), channel_id=1, source_target_pairs={{0,8},{8,16},{16,24},{24,0},{1,9},{9,17},{17,25},{25,1},{2,10},{10... | collective-permute-start | bytes 10616840 | tf_op jit(solution)/shard_map/ppermute | solution.py:18
  1575.0 36.3 %copy-start.12 = (f32[12,192,768]{2,1,0:T(8,128)S(1)}, f32[12,192,768]{2,1,0:T(8,128)}, u32[]{:S(2)}) copy-start(f32[12,192,768]{2,1,0:T(8,128)} %copy-done.11) | copy-start | bytes 21233668
  1575.0 36.3 %copy-start.16 = (f32[12,768,384]{2,1,0:T(8,128)S(1)}, f32[12,768,384]{2,1,0:T(8,128)}, u32[]{:S(2)}) copy-start(f32[12,768,384]{2,1,0:T(8,128)} %fusion.264) | copy-start | bytes 42467332
  1575.0 36.3 %copy-start.34 = (u16[768,384]{1,0:T(8,128)(2,1)S(1)}, u16[768,384]{1,0:T(8,128)(2,1)}, u32[]{:S(2)}) copy-start(u16[768,384]{1,0:T(8,128)(2,1)} %get-tuple-element.786) | copy-start | bytes 1769476
  1575.0 36.3 %copy-start.35 = (u16[768,384]{1,0:T(8,128)(2,1)S(1)}, u16[768,384]{1,0:T(8,128)(2,1)}, u32[]{:S(2)}) copy-start(u16[768,384]{1,0:T(8,128)(2,1)} %get-tuple-element.787) | copy-start | bytes 1769476
  1611.3 42.1 %collective-permute-start.3 = (bf16[12,192,768]{2,1,0:T(8,128)(2,1)}, bf16[12,192,768]{2,1,0:T(8,128)(2,1)S(1)}, u32[]{:S(2)}, u32[]{:S(2)}) collective-permute-start(bf16[12,192,768]{2,1,0:T(8,128)(2,1)} %fusion.244), channel_id=1, source_target_pairs={{0,8},{8,16},{16,24},{24,0},{1,9},{9,17},{17,25},{25,1},{2,10},{10... | collective-permute-start | bytes 10616840 | tf_op jit(solution)/shard_map/ppermute | solution.py:18
  1645.2 46.1 %collective-permute-start.2 = (bf16[12,192,768]{2,1,0:T(8,128)(2,1)S(1)}, bf16[12,192,768]{2,1,0:T(8,128)(2,1)S(1)}, u32[]{:S(2)}, u32[]{:S(2)}) collective-permute-start(bf16[12,192,768]{2,1,0:T(8,128)(2,1)S(1)} %fusion.245), channel_id=1, source_target_pairs={{0,8},{8,16},{16,24},{24,0},{1,9},{9,17},{17,25},{25,1},{2,10},{10... | collective-permute-start | bytes 10616840 | tf_op jit(solution)/shard_map/ppermute | solution.py:18
  (9 other events, 21.8 us)
where the time goes:
time: 1710 us; the launch traced here: 1700 us
  waiting for transfers between devices  554 us (32%)
  matrix products  298 us (17%)
  other arithmetic  291 us (17%)
  local copies, waits for them, and re-layouts  264 us (15%)
  blocking collectives  253 us (15%)
  starting transfers between devices  37.7 us (2%)
    all_to_all x1, blocking collectives, shards(): lax.all_to_all(mixed.reshape(sp_count * slots, half, width), 'sp', split_...  253 us
    all_to_all x4, waiting for transfers between devices, shards(): lax.all_to_all(grid_part[:, :, start:start + chunk].reshape(modes_dev, sp...  216 us
    ppermute x1, waiting for transfers between devices, shards(): other_weight = lax.ppermute(own_weight[half:], 'sp', partner)  191 us
    dot_general x4, matrix products, shards(): jnp.einsum('anh,ch->acn', hidden, down_weight[0], preferred_element_type=...  144 us
    reshape x8, local copies, waits for them, and re-layouts, shards(): on_grid.reshape(MMAX, chunk, 2, C)  90.3 us
    unnamed x104, local copies, waits for them, and re-layouts  87.1 us
    all_to_all x1, waiting for transfers between devices, shards(): lax.all_to_all(spectral, 'sp', split_axis=0, concat_axis=1, tiled=True)  71.5 us
    while x14, other arithmetic  69.9 us
  transfers between devices with their start and end apart: 11, of which 8 were waited for; matrix products, arithmetic and copies ran while one was open for 27% of the time, Pallas kernels for 0%

commit v1 on v0

--- a/solution.py
+++ b/solution.py
@@ -268,13 +268,10 @@
     chunk = cycle_rows // CHUNKS
     outputs = []
     for start in range(0, cycle_rows, chunk):
-        on_grid = lax.all_to_all(
-            grid_part[:, :, start : start + chunk].reshape(modes_dev, sp_count * chunk, width),
-            "sp",
-            split_axis=1,
-            concat_axis=0,
-            tiled=True,
-        )
+        part = grid_part[:, :, start : start + chunk].reshape(modes_dev, sp_count * chunk, width)
+        cells = jnp.split(part, lax.axis_size("sp"), axis=1)
+        arrived = lax.all_to_all(jnp.stack(cells), "sp", 0, 0)
+        on_grid = jnp.concatenate(arrived, axis=0)
         synthesis = jnp.einsum(
             "marc,rmn->acn",
             on_grid.reshape(MMAX, chunk, 2, C),

time: 1710 us -> 1720 us (level)
  local copies, waits for them, and re-layouts: 264 us -> 283 us
    another operation x0 -> x12, local copies, waits for them, and re-layouts: none -> 93.5 us  [the longest x8 90.3 us: shards(): on_grid.reshape(MMAX, chunk, 2, C)]
    reshape x8 -> x0, local copies, waits for them, and re-layouts: 90.3 us -> none  [shards(): on_grid.reshape(MMAX, chunk, 2, C)]
    unnamed x104 -> x132, local copies, waits for them, and re-layouts: 87.1 us -> 103 us
  transfers between devices with their start and end apart: 11 -> 11, of which waited for: 8 -> 8; matrix products, arithmetic and copies ran while one was open for 27% -> 28% of each run, Pallas kernels for 0% -> 0%
where the time goes in v1:
time: 1720 us; the launch traced here: 1710 us
  waiting for transfers between devices  540 us (31%)
  matrix products  298 us (17%)
  other arithmetic  291 us (17%)
  local copies, waits for them, and re-layouts  283 us (16%)
  blocking collectives  253 us (15%)
  starting transfers between devices  37.6 us (2%)
    all_to_all x1, blocking collectives, shards(): lax.all_to_all(mixed.reshape(sp_count * slots, half, width), 'sp', split_...  253 us
    all_to_all x4, waiting for transfers between devices, shards(): arrived = lax.all_to_all(jnp.stack(cells), 'sp', 0, 0)  202 us
    ppermute x1, waiting for transfers between devices, shards(): other_weight = lax.ppermute(own_weight[half:], 'sp', partner)  191 us
    dot_general x4, matrix products, shards(): jnp.einsum('anh,ch->acn', hidden, down_weight[0], preferred_element_type=...  144 us
    unnamed x132, local copies, waits for them, and re-layouts  103 us
    another operation x8, local copies, waits for them, and re-layouts, shards(): on_grid.reshape(MMAX, chunk, 2, C)  90.3 us
    all_to_all x1, waiting for transfers between devices, shards(): lax.all_to_all(spectral, 'sp', split_axis=0, concat_axis=1, tiled=True)  71.5 us
    while x14, other arithmetic  69.9 us
  transfers between devices with their start and end apart: 11, of which 8 were waited for; matrix products, arithmetic and copies ran while one was open for 28% of the time, Pallas kernels for 0%

profile of v1, /device:TPU:0, one launch (start us, length us, event | category | flops | bytes accessed | tf_op | source)
XLA Modules:
  0.0 1706.1 jit_solution(10296813555082019848)
XLA Ops:
  1.2 7.8 convert_reduce_fusion
  9.0 10.3 fusion.183
  24.8 19.0 %multiply_convert_fusion = bf16[48,192,2,384]{3,1,2,0:T(8,128)(2,1)} fusion(f32[48]{0:T(128)S(1)} %subtract_multiply_fusion, bf16[1,48,192,768]{3,2,1,0:T(8,128)(2,1)} %param.14, f32[192]{0:T(256)S(1)} %bitcast.764, f32[48,768]{1,0:T(8,128)S(1)} %add_rsqrt_fusion, f32[48,768]{1,0:T(8,128)S(1)} %broadcast_multiply_fusion, ...), kind=kOutput, calls=%fused_computation.485 | convolution fusion | flops 10923540480 | bytes 29787072 | tf_op jit(solution)/shard_map/nrm,acn->marc/dot_general | solution.py:201
  43.8 18.6 %copy.66 = bf16[384,48,384]{2,1,0:T(8,128)(2,1)} copy(bf16[384,48,384]{0,2,1:T(8,128)(2,1)} %bitcast.717) | data formatting | bytes 28311552 | tf_op jit(solution)/shard_map/reshape | solution.py:205
  62.4 7.3 all-to-all-start
  72.0 59.7 %while.70 = (s32[]{:T(128)}, f32[24,48,384]{2,1,0:T(8,128)}, f32[24,48,384]{2,1,0:T(8,128)}, f32[24,48,384]{2,1,0:T(8,128)}, f32[24,48,384]{2,1,0:T(8,128)}, /*i...) while((s32[]{:T(128)}, f32[24,48,384]{2,1,0:T(8,128)}, ...), condition=%wide.region_2.3_spmd.clone.clone, body=%wide.region_1.2_spmd.clone.clone.sunk | while | flops 123129520 | bytes 200388496 | solution.py:107
  132.4 58.0 %while.69 = (s32[]{:T(128)}, f32[48,384]{1,0:T(8,128)S(1)}, f32[48,384]{1,0:T(8,128)S(1)}, f32[48,384]{1,0:T(8,128)S(1)}, f32[24,48,384]{2,1,0:T(8,128)}, /*inde...) while((s32[]{:T(128)}, f32[48,384]{1,0:T(8,128)S(1)}, ...), condition=%wide.region_4.5_spmd.clone, body=%wide.region_3.4_spmd.clone.sunk | while | flops 368643 | bytes 1548453 | solution.py:123
  190.5 100.2 %while.68 = (s32[]{:T(128)}, f32[24,48,384]{2,1,0:T(8,128)}, f32[24,48,384]{2,1,0:T(8,128)}, f32[24,48,384]{2,1,0:T(8,128)S(1)}, bf16[2,8,24,48,384]{4,1,0,2,3:T...) while((s32[]{:T(128)}, f32[24,48,384]{2,1,0:T(8,128)}, ...), condition=%wide.region_6.7_spmd.clone.clone, body=%wide.region_5.6_spmd.clone.clone.sunk | while | flops 100568752 | bytes 101660528 | solution.py:140
  211.3 7.1 bitcast_dynamic-update-slice_fusion.25
  220.7 7.1 bitcast_dynamic-update-slice_fusion.27
  233.5 7.2 copy_dynamic-update-slice_fusion.2
  261.3 7.1 bitcast_dynamic-update-slice_fusion.25
  270.7 7.1 bitcast_dynamic-update-slice_fusion.27
  283.5 7.2 copy_dynamic-update-slice_fusion.2
  290.7 14.3 fusion.186
  305.0 71.5 %all-to-all-done = bf16[384,48,384]{2,1,0:T(8,128)(2,1)} async-done(((bf16[384,48,384]{2,1,0:T(8,128)(2,1)}), bf16[384,48,384]{2,1,0:T(8,128)(2,1)}, u32[]{:S(2)}, u32[]{:S(2)}) %all-to-all-start) | async-done | bytes 14155808 | tf_op jit(solution)/shard_map/all_to_all | solution.py:210
  376.5 12.9 copy.67
  389.4 19.7 %convolution_convert_fusion.1 = bf16[48,384,384]{2,1,0:T(8,128)(2,1)} fusion(bf16[48,384,384]{2,1,0:T(8,128)(2,1)} %fusion.186, bf16[48,384,384]{2,1,0:T(8,128)(2,1)} %bitcast.695), kind=kOutput, calls=%fused_computation.578 | convolution fusion | flops 5442895872 | bytes 42467328 | tf_op jit(solution)/shard_map/mla,mak->mlk/dot_general | solution.py:207
  453.3 191.3 %collective-permute-done = bf16[24,192,384]{2,1,0:T(8,128)(2,1)} collective-permute-done((bf16[24,192,384]{2,1,0:T(8,128)(2,1)}, bf16[24,192,384]{2,1,0:T(8,128)(2,1)}, u32[]{:S(2)}, u32[]{:S(2)}) %collective-permute-start) | collective-permute-done | bytes 3538976 | tf_op jit(solution)/shard_map/ppermute | solution.py:217
  655.4 29.7 %all-to-all-done.1 = bf16[408,24,384]{2,1,0:T(8,128)(2,1)} async-done(((bf16[408,24,384]{2,1,0:T(8,128)(2,1)}), bf16[408,24,384]{2,1,0:T(8,128)(2,1)}, u32[]{:S(2)}, u32[]{:S(2)}) %all-to-all-start.1) | async-done | bytes 7520288 | tf_op jit(solution)/shard_map/all_to_all | solution.py:230
  697.1 15.2 fusion.237
  712.3 8.9 convert_bitcast_fusion.1
  731.8 12.0 pad_select_fusion
  743.8 7.9 copy.70
  751.7 252.8 %all_to_all.48 = bf16[408,24,384]{2,1,0:T(8,128)(2,1)S(1)} all-to-all(bf16[408,24,384]{2,1,0:T(8,128)(2,1)S(1)} %bitcast.712), channel_id=1, replica_groups=mesh['section'=4,'sp'=8] {'sp'}, dimensions={0} | all-to-all | bytes 15040512 | tf_op jit(solution)/shard_map/all_to_all | solution.py:250
  1021.1 19.2 %convolution_convert_fusion = bf16[48,384,384]{2,1,0:T(8,128)(2,1)} fusion(bf16[48,384,384]{2,1,0:T(8,128)(2,1)} %fusion.186, bf16[48,384,384]{2,1,0:T(8,128)(2,1)} %fusion.307), kind=kOutput, calls=%fused_computation.577 | convolution fusion | flops 5442895872 | bytes 42467328 | tf_op jit(solution)/shard_map/mla,mlk->mak/dot_general | solution.py:264
  1040.3 14.2 fusion.514
  1079.2 67.2 %all-to-all-done.5 = bf16[8,48,12,384]{3,1,2,0:T(8,128)(2,1)} async-done(((bf16[8,48,12,384]{3,1,2,0:T(8,128)(2,1)}), bf16[8,48,12,384]{3,1,2,0:T(8,128)(2,1)}, u32[]{:S(2)}, u32[]{:S(2)}) %all-to-all-start.5) | async-done | bytes 3538976 | tf_op jit(solution)/shard_map/all_to_all | solution.py:273
  1161.8 67.6 %all-to-all-done.3 = bf16[8,48,12,384]{3,1,2,0:T(8,128)(2,1)} async-done(((bf16[8,48,12,384]{3,1,2,0:T(8,128)(2,1)}), bf16[8,48,12,384]{3,1,2,0:T(8,128)(2,1)}, u32[]{:S(2)}, u32[]{:S(2)}) %all-to-all-start.3) | async-done | bytes 3538976 | tf_op jit(solution)/shard_map/all_to_all | solution.py:273
  1244.9 67.6 %all-to-all-done.6 = bf16[8,48,12,384]{3,1,2,0:T(8,128)(2,1)} async-done(((bf16[8,48,12,384]{3,1,2,0:T(8,128)(2,1)}), bf16[8,48,12,384]{3,1,2,0:T(8,128)(2,1)}, u32[]{:S(2)}, u32[]{:S(2)}) %all-to-all-start.6) | async-done | bytes 3538976 | tf_op jit(solution)/shard_map/all_to_all | solution.py:273
  1322.6 9.5 copy.93
  1332.1 12.9 reshape.7109
  1345.1 9.5 copy.90
  1354.6 13.0 reshape.7106
  1367.6 9.5 copy.92
  1377.1 13.1 reshape.7108
  1418.6 9.5 copy.91
  1428.2 13.1 reshape.7107
  1451.1 6.9 fusion.264
  1464.5 6.9 fusion.266
  1471.4 32.9 %fusion.251 = (u16[768,384]{1,0:T(8,128)(2,1)S(1)}, u16[768,384]{1,0:T(8,128)(2,1)S(1)}, u16[768,384]{1,0:T(8,128)(2,1)S(1)}, u16[768,384]{1,0:T(8,128)(2,1)S(1)...) fusion(f32[384]{0:T(512)S(1)} %convert_reduce_fusion.1, ...), kind=kOutput, calls=%fused_computation.617 | convolution fusion | flops 1561853952 | bytes 68643072 | tf_op jit(solution)/shard_map/acn,ch->anh/dot_general | solution.py:283
  1504.3 37.1 %fusion.246 = bf16[12,192,768]{2,1,0:T(8,128)(2,1)} fusion(f32[12,192,768]{2,1,0:T(8,128)} %copy-done.21, f32[12,768,384]{2,1,0:T(8,128)} %get-tuple-element.1155, f32[384]{0:T(512)S(1)} %convert_reduce_fusion.1, u16[768,384]{1,0:T(8,128)(2,1)S(1)} %get-tuple-element.775, u16[768,384]{1,0:T(8,128)(2,1)S(1)} %get-tuple-element.774, ...), kind=kOutput, calls=%fused_computation.603 | convolution fusion | flops 1613758464 | bytes 26101248 | tf_op jit(solution)/shard_map/anh,ch->acn/dot_general | solution.py:287
  1541.4 37.0 %fusion.243 = bf16[12,192,768]{2,1,0:T(8,128)(2,1)} fusion(f32[12,192,768]{2,1,0:T(8,128)} %copy-done.8, f32[12,768,384]{2,1,0:T(8,128)S(1)} %copy-done.18, f32[384]{0:T(512)S(1)} %convert_reduce_fusion.1, u16[768,384]{1,0:T(8,128)(2,1)S(1)} %get-tuple-element.782, u16[768,384]{1,0:T(8,128)(2,1)S(1)} %get-tuple-element.783, ...), kind=kOutput, calls=%fused_computation.597 | convolution fusion | flops 1613758464 | bytes 26101248 | tf_op jit(solution)/shard_map/anh,ch->acn/dot_general | solution.py:287
  1580.0 36.2 %fusion.244 = bf16[12,192,768]{2,1,0:T(8,128)(2,1)} fusion(f32[12,192,768]{2,1,0:T(8,128)S(1)} %copy-done.10, f32[12,768,384]{2,1,0:T(8,128)S(1)} %copy-done.17, f32[384]{0:T(512)S(1)} %convert_reduce_fusion.1, u16[768,384]{1,0:T(8,128)(2,1)} %get-tuple-element.784, u16[768,384]{1,0:T(8,128)(2,1)} %get-tuple-element.785, ...), kind=kOutput, calls=%fused_computation.599 | convolution fusion | flops 1613758464 | bytes 26101248 | tf_op jit(solution)/shard_map/anh,ch->acn/dot_general | solution.py:287
  1616.3 33.9 %fusion.245 = bf16[12,192,768]{2,1,0:T(8,128)(2,1)S(1)} fusion(f32[12,192,768]{2,1,0:T(8,128)S(1)} %copy-done.12, f32[12,768,384]{2,1,0:T(8,128)S(1)} %copy-done.16, f32[384]{0:T(512)S(1)} %convert_reduce_fusion.1, u16[768,384]{1,0:T(8,128)(2,1)S(1)} %copy-done.34, u16[768,384]{1,0:T(8,128)(2,1)S(1)} %copy-done.35, bf16[1,192,384]{2,1,0:T(8,128)(2,1)S(1)} %copy-done.32), kind=kOutput, calls=%fused_computation.601 | convolution fusion | flops 1613758464 | bytes 26101248 | tf_op jit(solution)/shard_map/anh,ch->acn/dot_general | solution.py:287
  1650.8 7.5 collective-permute-done.3
  1658.3 37.9 %collective-permute-done.2 = bf16[12,192,768]{2,1,0:T(8,128)(2,1)S(1)} collective-permute-done((bf16[12,192,768]{2,1,0:T(8,128)(2,1)S(1)}, bf16[12,192,768]{2,1,0:T(8,128)(2,1)S(1)}, u32[]{:S(2)}, u32[]{:S(2)}) %collective-permute-start.2) | collective-permute-done | bytes 3538976 | tf_op jit(solution)/shard_map/ppermute | solution.py:18
  1696.2 9.6 maximum_bitcast_fusion
  (486 shorter events, 388.3 us)
Async XLA Ops:
  0.0 1451.1 %copy-start = (bf16[1,192,384]{2,1,0:T(8,128)(2,1)S(1)}, bf16[1,192,384]{2,1,0:T(8,128)(2,1)}, u32[]{:S(2)}) copy-start(bf16[1,192,384]{2,1,0:T(8,128)(2,1)} %param.18) | copy-start | bytes 442372
  0.0 70.3 %copy-start.25 = (s32[384]{0:T(512)}, s32[384]{0:T(512)S(1)}, u32[]{:S(2)}) copy-start(s32[384]{0:T(512)S(1)} %fusion.360) | copy-start | bytes 4612
  62.4 314.1 %all-to-all-start = ((bf16[384,48,384]{2,1,0:T(8,128)(2,1)}), bf16[384,48,384]{2,1,0:T(8,128)(2,1)}, u32[]{:S(2)}, u32[]{:S(2)}) async-start(bf16[384,48,384]{2,1,0:T(8,128)(2,1)} %copy.66), calls=%async_computation | async-start | bytes 28311552 | tf_op jit(solution)/shard_map/all_to_all | solution.py:210
  71.9 59.7 %copy-start.27 = (f32[384]{0:T(512)S(1)}, f32[384]{0:T(512)}, u32[]{:S(2)}) copy-start(f32[384]{0:T(512)} %sine_log_fusion) | copy-start | bytes 4612
  71.9 59.7 %copy-start.31 = (f32[48]{0:T(128)S(1)}, f32[48]{0:T(128)}, u32[]{:S(2)}) copy-start(f32[48]{0:T(128)} %add_multiply_fusion.16) | copy-start | bytes 580
  71.9 60.4 %copy-start.1 = (f32[24,48,384]{2,1,0:T(8,128)S(1)}, f32[24,48,384]{2,1,0:T(8,128)}, u32[]{:S(2)}) copy-start(f32[24,48,384]{2,1,0:T(8,128)} %custom-call.17) | copy-start | bytes 5308420
  71.9 60.4 %copy-start.19 = (f32[48,384]{1,0:T(8,128)S(1)}, f32[48,384]{1,0:T(8,128)}, u32[]{:S(2)}) copy-start(f32[48,384]{1,0:T(8,128)} %custom-call) | copy-start | bytes 221188
  72.0 60.4 %copy-start.20 = (f32[48,384]{1,0:T(8,128)S(1)}, f32[48,384]{1,0:T(8,128)}, u32[]{:S(2)}) copy-start(f32[48,384]{1,0:T(8,128)} %custom-call.1) | copy-start | bytes 221188
  87.6 4.4 copy-start.6
  96.6 3.9 copy-start.7
  101.5 5.5 copy-start.2
  101.5 5.5 copy-start.3
  101.5 5.5 copy-start.4
  101.5 5.5 copy-start.5
  118.6 4.4 copy-start.6
  127.7 3.9 copy-start.7
  190.4 100.2 %copy-start.24 = (pred[48,384]{1,0:T(8,128)(4,1)S(1)}, pred[48,384]{1,0:T(8,128)(4,1)}, u32[]{:S(2)}) copy-start(pred[48,384]{1,0:T(8,128)(4,1)} %iota_compare_fusion) | copy-start | bytes 55300
  438.5 246.6 %all-to-all-start.1 = ((bf16[408,24,384]{2,1,0:T(8,128)(2,1)}), bf16[408,24,384]{2,1,0:T(8,128)(2,1)}, u32[]{:S(2)}, u32[]{:S(2)}) async-start(bf16[408,24,384]{2,1,0:T(8,128)(2,1)} %slice_dynamic-update-slice_fusion.1), calls=%async_computation.1 | async-start | bytes 15040512 | tf_op jit(solution)/shard_map/all_to_all | solution.py:230
  443.4 8.8 copy-start.33
  447.5 197.0 %collective-permute-start = (bf16[24,192,384]{2,1,0:T(8,128)(2,1)}, bf16[24,192,384]{2,1,0:T(8,128)(2,1)}, u32[]{:S(2)}, u32[]{:S(2)}) collective-permute-start(bf16[24,192,384]{2,1,0:T(8,128)(2,1)} %slice_bitcast_fusion), channel_id=1, source_target_pairs={{0,7},{1,6},{2,5},{3,4},{4,3},{5,2},{6,1},{7,0},{8,15},{9,14},{10,... | collective-permute-start | bytes 10616840 | tf_op jit(solution)/shard_map/ppermute | solution.py:217
  1063.2 83.2 %all-to-all-start.5 = ((bf16[8,48,12,384]{3,1,2,0:T(8,128)(2,1)}), bf16[8,48,12,384]{3,1,2,0:T(8,128)(2,1)}, u32[]{:S(2)}, u32[]{:S(2)}) async-start(bf16[8,48,12,384]{3,1,2,0:T(8,128)(2,1)} %fusion.316), calls=%async_computation.5 | async-start | bytes 7077888 | tf_op jit(solution)/shard_map/all_to_all | solution.py:273
  1146.4 83.1 %all-to-all-start.3 = ((bf16[8,48,12,384]{3,1,2,0:T(8,128)(2,1)}), bf16[8,48,12,384]{3,1,2,0:T(8,128)(2,1)}, u32[]{:S(2)}, u32[]{:S(2)}) async-start(bf16[8,48,12,384]{3,1,2,0:T(8,128)(2,1)} %fusion.332), calls=%async_computation.3 | async-start | bytes 7077888 | tf_op jit(solution)/shard_map/all_to_all | solution.py:273
  1229.4 83.1 %all-to-all-start.6 = ((bf16[8,48,12,384]{3,1,2,0:T(8,128)(2,1)}), bf16[8,48,12,384]{3,1,2,0:T(8,128)(2,1)}, u32[]{:S(2)}, u32[]{:S(2)}) async-start(bf16[8,48,12,384]{3,1,2,0:T(8,128)(2,1)} %fusion.308), calls=%async_computation.6 | async-start | bytes 7077888 | tf_op jit(solution)/shard_map/all_to_all | solution.py:273
  1244.9 72.1 %copy-start.30 = (bf16[1,192]{1,0:T(2,128)(2,1)S(1)}, bf16[1,192]{1,0:T(2,128)(2,1)}, u32[]{:S(2)}) copy-start(bf16[1,192]{1,0:T(2,128)(2,1)} %param.17) | copy-start | bytes 1156
  1244.9 72.1 %copy-start.29 = (bf16[1,384]{1,0:T(2,128)(2,1)S(1)}, bf16[1,384]{1,0:T(2,128)(2,1)}, u32[]{:S(2)}) copy-start(bf16[1,384]{1,0:T(2,128)(2,1)} %param.19) | copy-start | bytes 2308
  1244.9 72.1 %copy-start.26 = (s32[384]{0:T(512)S(1)}, s32[384]{0:T(512)}, u32[]{:S(2)}) copy-start(s32[384]{0:T(512)} %copy-done.25) | copy-start | bytes 4612
  1312.5 106.1 %all-to-all-start.4 = ((bf16[8,48,12,384]{3,1,2,0:T(8,128)(2,1)}), bf16[8,48,12,384]{3,1,2,0:T(8,128)(2,1)}, u32[]{:S(2)}, u32[]{:S(2)}) async-start(bf16[8,48,12,384]{3,1,2,0:T(8,128)(2,1)} %fusion.324), calls=%async_computation.4 | async-start | bytes 7077888 | tf_op jit(solution)/shard_map/all_to_all | solution.py:273
  1396.4 3.6 copy-start.8
  1396.4 4.6 copy-start.23
  1406.1 3.6 copy-start.21
  1406.1 4.6 copy-start.22
  1447.5 3.6 copy-start.11
  1447.5 10.4 slice-start.2
  1451.1 6.9 slice-start.3
  1451.1 13.4 slice-start
  1458.0 6.5 slice-start.1
  1471.4 32.9 %copy-start.32 = (bf16[1,192,384]{2,1,0:T(8,128)(2,1)S(1)}, bf16[1,192,384]{2,1,0:T(8,128)(2,1)}, u32[]{:S(2)}) copy-start(bf16[1,192,384]{2,1,0:T(8,128)(2,1)} %param.20) | copy-start | bytes 442372
  1504.3 37.1 %copy-start.18 = (f32[12,768,384]{2,1,0:T(8,128)S(1)}, f32[12,768,384]{2,1,0:T(8,128)}, u32[]{:S(2)}) copy-start(f32[12,768,384]{2,1,0:T(8,128)} %fusion.266) | copy-start | bytes 42467332
  1541.4 109.5 %collective-permute-start.1 = (bf16[12,192,768]{2,1,0:T(8,128)(2,1)}, bf16[12,192,768]{2,1,0:T(8,128)(2,1)}, u32[]{:S(2)}, u32[]{:S(2)}) collective-permute-start(bf16[12,192,768]{2,1,0:T(8,128)(2,1)} %fusion.246), channel_id=1, source_target_pairs={{0,8},{8,16},{16,24},{24,0},{1,9},{9,17},{17,25},{25,1},{2,10},{10... | collective-permute-start | bytes 10616840 | tf_op jit(solution)/shard_map/ppermute | solution.py:18
  1541.4 38.6 %copy-start.10 = (f32[12,192,768]{2,1,0:T(8,128)S(1)}, f32[12,192,768]{2,1,0:T(8,128)}, u32[]{:S(2)}) copy-start(f32[12,192,768]{2,1,0:T(8,128)} %copy-done.9) | copy-start | bytes 21233668
  1541.4 38.6 %copy-start.17 = (f32[12,768,384]{2,1,0:T(8,128)S(1)}, f32[12,768,384]{2,1,0:T(8,128)}, u32[]{:S(2)}) copy-start(f32[12,768,384]{2,1,0:T(8,128)} %fusion.265) | copy-start | bytes 42467332
  1578.4 72.5 %collective-permute-start.4 = (bf16[12,192,768]{2,1,0:T(8,128)(2,1)}, bf16[12,192,768]{2,1,0:T(8,128)(2,1)}, u32[]{:S(2)}, u32[]{:S(2)}) collective-permute-start(bf16[12,192,768]{2,1,0:T(8,128)(2,1)} %fusion.243), channel_id=1, source_target_pairs={{0,8},{8,16},{16,24},{24,0},{1,9},{9,17},{17,25},{25,1},{2,10},{10... | collective-permute-start | bytes 10616840 | tf_op jit(solution)/shard_map/ppermute | solution.py:18
  1580.0 36.3 %copy-start.12 = (f32[12,192,768]{2,1,0:T(8,128)S(1)}, f32[12,192,768]{2,1,0:T(8,128)}, u32[]{:S(2)}) copy-start(f32[12,192,768]{2,1,0:T(8,128)} %copy-done.11) | copy-start | bytes 21233668
  1580.0 36.3 %copy-start.16 = (f32[12,768,384]{2,1,0:T(8,128)S(1)}, f32[12,768,384]{2,1,0:T(8,128)}, u32[]{:S(2)}) copy-start(f32[12,768,384]{2,1,0:T(8,128)} %fusion.264) | copy-start | bytes 42467332
  1580.0 36.3 %copy-start.34 = (u16[768,384]{1,0:T(8,128)(2,1)S(1)}, u16[768,384]{1,0:T(8,128)(2,1)}, u32[]{:S(2)}) copy-start(u16[768,384]{1,0:T(8,128)(2,1)} %get-tuple-element.786) | copy-start | bytes 1769476
  1580.0 36.3 %copy-start.35 = (u16[768,384]{1,0:T(8,128)(2,1)S(1)}, u16[768,384]{1,0:T(8,128)(2,1)}, u32[]{:S(2)}) copy-start(u16[768,384]{1,0:T(8,128)(2,1)} %get-tuple-element.787) | copy-start | bytes 1769476
  1616.2 42.1 %collective-permute-start.3 = (bf16[12,192,768]{2,1,0:T(8,128)(2,1)}, bf16[12,192,768]{2,1,0:T(8,128)(2,1)S(1)}, u32[]{:S(2)}, u32[]{:S(2)}) collective-permute-start(bf16[12,192,768]{2,1,0:T(8,128)(2,1)} %fusion.244), channel_id=1, source_target_pairs={{0,8},{8,16},{16,24},{24,0},{1,9},{9,17},{17,25},{25,1},{2,10},{10... | collective-permute-start | bytes 10616840 | tf_op jit(solution)/shard_map/ppermute | solution.py:18
  1650.2 46.1 %collective-permute-start.2 = (bf16[12,192,768]{2,1,0:T(8,128)(2,1)S(1)}, bf16[12,192,768]{2,1,0:T(8,128)(2,1)S(1)}, u32[]{:S(2)}, u32[]{:S(2)}) collective-permute-start(bf16[12,192,768]{2,1,0:T(8,128)(2,1)S(1)} %fusion.245), channel_id=1, source_target_pairs={{0,8},{8,16},{16,24},{24,0},{1,9},{9,17},{17,25},{25,1},{2,10},{10... | collective-permute-start | bytes 10616840 | tf_op jit(solution)/shard_map/ppermute | solution.py:18
  (9 other events, 21.8 us)
